TPU v7x, 32 devices: a whole 2x2x4 slice. The times are simulated.
32 devices in a mesh: row: 4 (over y, x), orb: 8 (over z, core).
Axes of the slice: x: 2, y: 2, z: 4, core: 2. Of those that a mesh axis runs over, the one named last changes fastest.
Arguments:
- integrals: bfloat16 [24, 1024, 5120], P('orb', 'row'), may hold values from -6 to 6
- tile_ids: int32 [8, 40], P('row'), may hold values from 0 to 127, as said below
- coefficients: bfloat16 [1024, 16384], P('orb'), may hold values from -0.078125 to 0.078125
- metric: float32 [24, 24], replicated, may hold values from -0.0078125 to 0.0078125
Outputs:
- exchange_columns: float32 [1024, 1024], P('orb', 'row')
Inputs may be any that keep to these rules, and one draw needn't show every extreme that they name: `tile_ids`: row block b covers basis functions b * 128 to b * 128 + 127. Each row lists 40 different column tiles (tile t covers basis functions t * 128 to t * 128 + 127); the first is the block's own tile b.
All inputs are finite; a program needn't handle non-finite values.
Results may differ from a plain program's by a relative error of at most 0.022.
Values may be sent and summed in bfloat16 or wider, within the bound.
A program may use at most 128 MiB of HBM per device.

v0:
```python
import jax
import jax.numpy as jnp
from jax import lax
from jax.sharding import PartitionSpec as P


def per_device(integrals, tile_ids, coefficients, metric):
    aux_local, local_rows, kept_width = integrals.shape
    orb_local, basis_width = coefficients.shape
    block_count, kept_count = tile_ids.shape
    tile_rows = local_rows // block_count
    blocked = coefficients.reshape(orb_local, basis_width // tile_rows, tile_rows)
    picked = jnp.take(blocked, tile_ids.reshape(block_count * kept_count), axis=1)
    picked = picked.reshape(orb_local, block_count, kept_count * tile_rows)
    slabs = integrals.reshape(aux_local, block_count, tile_rows, kept_width)
    col_piece = lax.all_gather(picked, "orb", axis=0, tiled=True)
    halves = jnp.einsum("pbmk,jbk->pjbm", slabs, col_piece, preferred_element_type=jnp.float32)
    halves = halves.reshape(aux_local, col_piece.shape[0], local_rows).astype(jnp.bfloat16)
    own_piece = col_piece[:, :, :tile_rows].reshape(col_piece.shape[0], local_rows)
    stacked = jnp.concatenate([halves, own_piece[None]], axis=0)
    halves = stacked[:aux_local]
    own_rows = stacked[aux_local]
    by_orbital = lax.all_to_all(halves, "orb", split_axis=1, concat_axis=0, tiled=True)
    partial_sum = jnp.einsum(
        "qjm,im->qji", by_orbital, own_rows, preferred_element_type=jnp.float32
    )
    occupied_share = lax.psum_scatter(
        partial_sum.astype(jnp.bfloat16), "row", scatter_dimension=2, tiled=True
    ).astype(jnp.float32)
    fitted_share = jnp.einsum(
        "pq,qji->pji", metric, occupied_share, precision=lax.Precision.HIGHEST
    ).astype(jnp.bfloat16)
    fitted = lax.all_gather(fitted_share, "row", axis=2, tiled=True)
    return lax.psum_scatter(
        jnp.einsum("pjm,pji->im", by_orbital, fitted, preferred_element_type=jnp.float32).astype(
            jnp.bfloat16
        ),
        "orb",
        scatter_dimension=0,
        tiled=True,
    ).astype(jnp.float32)


def solution(mesh):
    return jax.shard_map(
        per_device,
        mesh=mesh,
        in_specs=(P("orb", "row", None), P("row", None), P("orb", None), P()),
        out_specs=P("orb", "row"),
        check_vma=False,
    )
```

profile of v0, /device:TPU:0, one launch (start us, length us, event | category | flops | bytes accessed | tf_op | source)
XLA Modules:
  0.0 483.4 jit_solution(17122439805342675751)
XLA Ops:
  6.5 0.8 reshape.51
  7.3 0.7 compare_and_fusion
  8.1 6.4 %copy.25 = bf16[128,16384]{0,1:T(8,128)(2,1)} copy(bf16[128,16384]{1,0:T(8,128)(2,1)} %param.6) | data formatting | bytes 8388608 | tf_op args[2]
  14.5 6.4 %copy.26 = bf16[128,128,128]{2,0,1:T(8,128)(2,1)} copy(bf16[128,128,128]{0,2,1:T(8,128)(2,1)} %bitcast.42) | data formatting | bytes 8388608 | tf_op jit(solution)/shard_map/reshape | solution.py:12
  20.9 3.2 gather_fusion
  24.2 2.6 copy.27
  26.7 3.0 copy.28
  29.7 1.8 broadcast_select_fusion
  31.6 188.3 %all-gather.3.cloned.1.call-done = bf16[1024,2,5120]{2,0,1:T(8,128)(2,1)} async-done(((bf16[128,2,5120]{2,0,1:T(8,128)(2,1)}), bf16[1024,2,5120]{2,0,1:T(8,128)(2,1)}) %all-gather.3.cloned.1.call-update) | async-done | bytes 20971536 | tf_op jit(solution)/shard_map/all_gather | solution.py:16
  219.9 14.0 %fusion.11 = bf16[3,1024,2,128]{1,3,0,2:T(8,128)(2,1)S(1)} fusion(bf16[3,2,128,5120]{3,2,1,0:T(8,128)(2,1)} %bitcast.51, bf16[1024,2,5120]{2,0,1:T(8,128)(2,1)} %all-gather.3.cloned.1.call-done), kind=kOutput, calls=%fused_computation.11 | convolution fusion | flops 8053850112 | bytes 30408704 | tf_op jit(solution)/shard_map/pbmk,jbk->pjbm/dot_general | solution.py:17
  233.9 0.2 copy.30
  234.1 2.6 copy.31
  236.6 3.7 all-to-all-start
  240.4 0.2 copy.34
  240.7 48.7 %all-to-all-done = bf16[3,1024,256]{2,0,1:T(4,128)(2,1)S(1)} async-done(((bf16[3,1024,256]{2,0,1:T(4,128)(2,1)}), bf16[3,1024,256]{2,0,1:T(4,128)(2,1)S(1)}, u32[]{:S(2)}, u32[]{:S(2)}) %all-to-all-start) | async-done | bytes 1572896 | tf_op jit(solution)/shard_map/all_to_all | solution.py:23
  289.3 0.2 copy.32
  289.6 0.1 copy.33
  289.7 4.5 convolution_convert_fusion
  294.2 69.0 %reduce-scatter.3.cloned.1.call-done = bf16[24,128,256]{2,1,0:T(8,128)(2,1)} async-done(((bf16[24,128,1024]{2,1,0:T(8,128)(2,1)}), bf16[24,128,256]{2,1,0:T(8,128)(2,1)}) %reduce-scatter.3.cloned.1.call-update) | async-done | bytes 1572880 | tf_op jit(solution)/shard_map/reduce_scatter | solution.py:27
  363.2 4.5 fusion.16
  367.8 70.0 %all-gather.5.cloned.1.call-done = bf16[24,128,1024]{2,0,1:T(8,128)(2,1)} async-done(((bf16[24,128,256]{2,0,1:T(8,128)(2,1)}), bf16[24,128,1024]{2,0,1:T(8,128)(2,1)}) %all-gather.5.cloned.1.call-update) | async-done | bytes 6291472 | tf_op jit(solution)/shard_map/all_gather | solution.py:33
  437.8 6.0 %fusion.22 = bf16[1024,256]{1,0:T(8,128)(2,1)} fusion(bf16[24,128,1024]{2,0,1:T(8,128)(2,1)} %all-gather.5.cloned.1.call-done, bf16[24,128,256]{2,1,0:T(8,128)(2,1)S(1)} %bitcast.46), kind=kOutput, calls=%fused_computation.14 | convolution fusion | flops 1610874880 | bytes 8388608 | tf_op jit(solution)/shard_map/pjm,pji->im/dot_general | solution.py:35
  443.8 31.6 %reduce-scatter.5.cloned.1.call-done = bf16[128,256]{1,0:T(8,128)(2,1)} async-done(((bf16[1024,256]{1,0:T(8,128)(2,1)}), bf16[128,256]{1,0:T(8,128)(2,1)}) %reduce-scatter.5.cloned.1.call-update) | async-done | bytes 65552 | tf_op jit(solution)/shard_map/reduce_scatter | solution.py:34
  475.4 1.5 convert_element_type.32
  (16 shorter events, 0.3 us)
Async XLA Ops:
  6.5 356.6 %copy-start = (f32[24,24]{1,0:T(8,128)S(1)}, f32[24,24]{1,0:T(8,128)}, u32[]{:S(2)}) copy-start(f32[24,24]{1,0:T(8,128)} %param.7) | copy-start | bytes 6916
  6.5 213.4 %all-gather.3.cloned.1.call-start = ((), (), s32[]{:S(2)}) async-start(), calls=%async_computation.3 | async-start | bytes 23592960 | tf_op jit(solution)/shard_map/all_gather | solution.py:16
  236.6 3.8 slice-start
  236.6 52.7 %all-to-all-start = ((bf16[3,1024,256]{2,0,1:T(4,128)(2,1)}), bf16[3,1024,256]{2,0,1:T(4,128)(2,1)S(1)}, u32[]{:S(2)}, u32[]{:S(2)}) async-start(bf16[3,1024,256]{2,0,1:T(4,128)(2,1)} %copy.31), calls=%async_computation | async-start | bytes 4194304 | tf_op jit(solution)/shard_map/all_to_all | solution.py:23
  240.4 122.8 %reduce-scatter.3.cloned.1.call-start = ((), (), s32[]{:S(2)}) async-start(), calls=%async_computation.4 | async-start | bytes 7864320 | tf_op jit(solution)/shard_map/reduce_scatter | solution.py:27
  294.2 143.6 %all-gather.5.cloned.1.call-start = ((), (), s32[]{:S(2)}) async-start(), calls=%async_computation.5 | async-start | bytes 7864320 | tf_op jit(solution)/shard_map/all_gather | solution.py:33
  367.7 107.6 %reduce-scatter.5.cloned.1.call-start = ((), (), s32[]{:S(2)}) async-start(), calls=%async_computation.6 | async-start | bytes 589824 | tf_op jit(solution)/shard_map/reduce_scatter | solution.py:34
Sparse Core Ops, SparseCore 0:
  31.7 188.1 all-gather.2
  294.3 68.8 reduce-scatter.2
  367.8 69.8 all-gather.4
  443.9 31.4 reduce-scatter.4
where the time goes:
time: 484 us; the launch traced here: 483 us
  waiting for transfers between devices  408 us (84%)
  matrix products  28.9 us (6%)
  local copies, waits for them, and re-layouts  25.8 us (5%)
  between operations  13.2 us (3%)
    all_gather x1, waiting for transfers between devices, per_device(): col_piece = lax.all_gather(picked, 'orb', axis=0, tiled=True)  188 us
    all_gather x1, waiting for transfers between devices, per_device(): fitted = lax.all_gather(fitted_share, 'row', axis=2, tiled=True)  70 us
    reduce_scatter x1, waiting for transfers between devices, per_device(): lax.psum_scatter(partial_sum.astype(jnp.bfloat16), 'row', scatter_dimensi...  69 us
    all_to_all x1, waiting for transfers between devices, per_device(): lax.all_to_all(halves, 'orb', split_axis=1, concat_axis=0, tiled=True)  48.7 us
    reduce_scatter x1, waiting for transfers between devices, per_device(): lax.psum_scatter(jnp.einsum('pjm,pji->im', by_orbital, fitted, preferred_...  31.6 us
    dot_general x1, matrix products, per_device(): jnp.einsum('pbmk,jbk->pjbm', slabs, col_piece, preferred_element_type=jnp...  14 us
  transfers between devices with their start and end apart: 5, of which 5 were waited for; matrix products, arithmetic and copies ran while one was open for 0% of the time, Pallas kernels for 0%

commit v1 on v0

--- a/solution.py
+++ b/solution.py
@@ -2,6 +2,13 @@
 import jax.numpy as jnp
 from jax import lax
 from jax.sharding import PartitionSpec as P
+from jax.lax import all_to_all, psum
+
+
+def show_cells(s0, net_axis):
+    return jnp.concatenate(
+        all_to_all(jnp.stack(jnp.split(s0, psum(1, net_axis), 1)), net_axis, 0, 0), 0
+    )
 
 
 def per_device(integrals, tile_ids, coefficients, metric):
@@ -20,7 +27,7 @@
     stacked = jnp.concatenate([halves, own_piece[None]], axis=0)
     halves = stacked[:aux_local]
     own_rows = stacked[aux_local]
-    by_orbital = lax.all_to_all(halves, "orb", split_axis=1, concat_axis=0, tiled=True)
+    by_orbital = show_cells(halves, "orb")
     partial_sum = jnp.einsum(
         "qjm,im->qji", by_orbital, own_rows, preferred_element_type=jnp.float32
     )

time: 484 us -> 475 us (0.981)
  waiting for transfers between devices: 408 us -> 395 us
    all_to_all x1, waiting for transfers between devices: 48.7 us -> 37.4 us  [show_cells(): all_to_all(jnp.stack(jnp.split(s0, psum(1, net_axis), 1)), net_axis, 0, 0)]
    unnamed x5 -> x12, local copies, waits for them, and re-layouts: 6.48 us -> 11.6 us
where the time goes in v1:
time: 475 us
  waiting for transfers between devices  395 us (83%)
  local copies, waits for them, and re-layouts  29.8 us (6%)
  matrix products  28.4 us (6%)
  between operations  13.2 us (3%)
    all_gather x1, waiting for transfers between devices, per_device(): col_piece = lax.all_gather(picked, 'orb', axis=0, tiled=True)  188 us
    reduce_scatter x1, waiting for transfers between devices, per_device(): lax.psum_scatter(partial_sum.astype(jnp.bfloat16), 'row', scatter_dimensi...  69 us
    all_gather x1, waiting for transfers between devices, per_device(): fitted = lax.all_gather(fitted_share, 'row', axis=2, tiled=True)  68.7 us
    all_to_all x1, waiting for transfers between devices, show_cells(): all_to_all(jnp.stack(jnp.split(s0, psum(1, net_axis), 1)), net_axis, 0, 0)  37.4 us
    reduce_scatter x1, waiting for transfers between devices, per_device(): lax.psum_scatter(jnp.einsum('pjm,pji->im', by_orbital, fitted, preferred_...  31.6 us
    dot_general x1, matrix products, per_device(): jnp.einsum('pbmk,jbk->pjbm', slabs, col_piece, preferred_element_type=jnp...  14 us
    unnamed x12, local copies, waits for them, and re-layouts  11.6 us
  transfers between devices with their start and end apart: 5, of which 5 were waited for; matrix products, arithmetic and copies ran while one was open for 0% of the time, Pallas kernels for 0%

profile of v1, /device:TPU:0, one launch (start us, length us, event | category | flops | bytes accessed | tf_op | source)
XLA Modules:
  0.0 474.5 jit_solution(1691613782057357635)
XLA Ops:
  6.5 0.8 reshape.54
  8.1 6.4 %copy.12 = bf16[128,16384]{0,1:T(8,128)(2,1)} copy(bf16[128,16384]{1,0:T(8,128)(2,1)} %param.6) | data formatting | bytes 8388608 | tf_op args[2]
  14.5 6.4 %copy.13 = bf16[128,128,128]{2,0,1:T(8,128)(2,1)} copy(bf16[128,128,128]{0,2,1:T(8,128)(2,1)} %bitcast.74) | data formatting | bytes 8388608 | tf_op jit(solution)/shard_map/reshape | solution.py:19
  20.9 3.2 gather_fusion
  24.2 2.6 copy.14
  26.7 3.0 copy.15
  29.7 1.8 broadcast_select_fusion
  31.6 188.3 %all-gather.3.cloned.1.call-done = bf16[1024,2,5120]{2,0,1:T(8,128)(2,1)} async-done(((bf16[128,2,5120]{2,0,1:T(8,128)(2,1)}), bf16[1024,2,5120]{2,0,1:T(8,128)(2,1)}) %all-gather.3.cloned.1.call-update) | async-done | bytes 20971536 | tf_op jit(solution)/shard_map/all_gather | solution.py:23
  219.9 14.0 %fusion.9 = bf16[3,1024,2,128]{1,3,0,2:T(8,128)(2,1)S(1)} fusion(bf16[3,2,128,5120]{3,2,1,0:T(8,128)(2,1)} %bitcast.89, bf16[1024,2,5120]{2,0,1:T(8,128)(2,1)} %all-gather.3.cloned.1.call-done), kind=kOutput, calls=%fused_computation.9 | convolution fusion | flops 8053850112 | bytes 30408704 | tf_op jit(solution)/shard_map/pbmk,jbk->pjbm/dot_general | solution.py:24
  234.7 0.7 fusion.24
  236.2 0.7 fusion.22
  236.9 0.7 fusion.21
  238.4 0.7 fusion.19
  239.1 0.7 fusion.18
  239.8 3.7 all-to-all-start
  243.9 37.4 %all-to-all-done = bf16[8,3,128,256]{2,3,1,0:T(8,128)(2,1)S(1)} async-done(((bf16[8,3,128,256]{2,3,1,0:T(8,128)(2,1)}), bf16[8,3,128,256]{2,3,1,0:T(8,128)(2,1)S(1)}, u32[]{:S(2)}, u32[]{:S(2)}) %all-to-all-start) | async-done | bytes 1572896 | tf_op jit(solution)/shard_map/all_to_all | solution.py:10
  281.3 4.5 convolution_convert_fusion
  285.9 69.0 %reduce-scatter.3.cloned.1.call-done = bf16[24,128,256]{2,1,0:T(8,128)(2,1)} async-done(((bf16[24,128,1024]{2,1,0:T(8,128)(2,1)}), bf16[24,128,256]{2,1,0:T(8,128)(2,1)}) %reduce-scatter.3.cloned.1.call-update) | async-done | bytes 1572880 | tf_op jit(solution)/shard_map/reduce_scatter | solution.py:34
  354.8 4.5 fusion.14
  359.6 1.1 copy.26
  360.7 68.7 %all-gather.5.cloned.1.call-done = bf16[24,128,1024]{2,0,1:T(8,128)(2,1)} async-done(((bf16[24,128,256]{2,0,1:T(8,128)(2,1)}), bf16[24,128,1024]{2,0,1:T(8,128)(2,1)}) %all-gather.5.cloned.1.call-update) | async-done | bytes 6291472 | tf_op jit(solution)/shard_map/all_gather | solution.py:40
  429.4 5.5 %fusion.17 = bf16[1024,256]{1,0:T(8,128)(2,1)} fusion(bf16[24,128,1024]{2,0,1:T(8,128)(2,1)} %all-gather.5.cloned.1.call-done, bf16[24,128,256]{2,0,1:T(8,128)(2,1)S(1)} %copy.26), kind=kOutput, calls=%fused_computation.12 | convolution fusion | flops 1610874880 | bytes 8388608 | tf_op jit(solution)/shard_map/pjm,pji->im/dot_general | solution.py:42
  434.9 31.6 %reduce-scatter.5.cloned.1.call-done = bf16[128,256]{1,0:T(8,128)(2,1)} async-done(((bf16[1024,256]{1,0:T(8,128)(2,1)}), bf16[128,256]{1,0:T(8,128)(2,1)}) %reduce-scatter.5.cloned.1.call-update) | async-done | bytes 65552 | tf_op jit(solution)/shard_map/reduce_scatter | solution.py:41
  466.5 1.5 convert_element_type.32
  (22 shorter events, 3.7 us)
Async XLA Ops:
  6.5 348.3 %copy-start = (f32[24,24]{1,0:T(8,128)S(1)}, f32[24,24]{1,0:T(8,128)}, u32[]{:S(2)}) copy-start(f32[24,24]{1,0:T(8,128)} %param.7) | copy-start | bytes 6916
  6.5 213.4 %all-gather.3.cloned.1.call-start = ((), (), s32[]{:S(2)}) async-start(), calls=%async_computation.3 | async-start | bytes 23592960 | tf_op jit(solution)/shard_map/all_gather | solution.py:23
  239.8 3.8 slice-start
  239.8 41.4 %all-to-all-start = ((bf16[8,3,128,256]{2,3,1,0:T(8,128)(2,1)}), bf16[8,3,128,256]{2,3,1,0:T(8,128)(2,1)S(1)}, u32[]{:S(2)}, u32[]{:S(2)}) async-start(bf16[8,3,128,256]{2,3,1,0:T(8,128)(2,1)} %fusion.18), calls=%async_computation | async-start | bytes 3145728 | tf_op jit(solution)/shard_map/all_to_all | solution.py:10
  243.6 111.3 %reduce-scatter.3.cloned.1.call-start = ((), (), s32[]{:S(2)}) async-start(), calls=%async_computation.4 | async-start | bytes 7864320 | tf_op jit(solution)/shard_map/reduce_scatter | solution.py:34
  285.8 143.6 %all-gather.5.cloned.1.call-start = ((), (), s32[]{:S(2)}) async-start(), calls=%async_computation.5 | async-start | bytes 7864320 | tf_op jit(solution)/shard_map/all_gather | solution.py:40
  359.4 107.1 %reduce-scatter.5.cloned.1.call-start = ((), (), s32[]{:S(2)}) async-start(), calls=%async_computation.6 | async-start | bytes 589824 | tf_op jit(solution)/shard_map/reduce_scatter | solution.py:41
Sparse Core Ops, SparseCore 0:
  31.7 188.1 all-gather.2
  285.9 68.8 reduce-scatter.2
  359.5 69.8 all-gather.4
  435.0 31.3 reduce-scatter.4
